TPU v7x, 32 devices: a whole 2x2x4 slice. The times are simulated.
32 devices in a mesh: dp: 8 (over y, x, core), mp: 4 (over z).
Axes of the slice: x: 2, y: 2, z: 4, core: 2. Of those that a mesh axis runs over, the one named last changes fastest.
Arguments:
- tokens: bfloat16 [8192, 1024], P('dp'), may hold values from -30 to 30
- query_key_value_weight: bfloat16 [1024, 3072], P(None, 'mp'), may hold values from -0.1875 to 0.1875
- adapter_down_weight: bfloat16 [1024, 512], P(None, 'mp'), may hold values from -0.1875 to 0.1875
- adapter_up_weight: bfloat16 [512, 3072], P('mp'), may hold values from -0.75 to 0.75
- attention_out_weight: bfloat16 [1024, 1024], P('mp'), may hold values from -0.1875 to 0.1875
- first_norm_gain: float32 [1024], replicated, may hold values from 0.5 to 1.5
- first_norm_bias: float32 [1024], replicated, may hold values from -3 to 3
- first_feed_weight: bfloat16 [1024, 4096], P(None, 'mp'), may hold values from -0.1875 to 0.1875
- first_feed_bias: float32 [4096], P('mp'), may hold values from -3 to 3
- second_feed_weight: bfloat16 [4096, 1024], P('mp'), may hold values from -0.09375 to 0.09375
- second_feed_bias: float32 [1024], replicated, may hold values from -3 to 3
- second_norm_gain: float32 [1024], replicated, may hold values from 0.5 to 1.5
- second_norm_bias: float32 [1024], replicated, may hold values from -3 to 3
- following_qkv_weight: bfloat16 [1024, 3072], P(None, 'mp'), may hold values from -0.1875 to 0.1875
- following_bias: float32 [3072], P('mp'), may hold values from -3 to 3
- request_page_count: int32 [4], replicated, may hold values from 1 to 32, 64 in all
- page_slot_table: int32 [64], replicated, may hold values from 0 to 63, each once
- request_adapter: int32 [4], replicated, may hold values from 0 to 31, as said below
Outputs:
- layer_out: bfloat16 [8192, 1024], P(('dp', 'mp'))
- next_qkv: bfloat16 [8192, 3072], P('dp', 'mp')
Inputs may be any that keep to these rules, and one draw needn't show every extreme that they name: `request_page_count`: the counts sum to 64; the longest request has exactly 32 pages. `page_slot_table`: names every page slot once. `request_adapter`: exactly min(16, 4) distinct adapters are named, adapters 0 and 31 among them; of the 8 adapters held by one index of mp at most 1 are named, and some index holds exactly 1 named ones.
All inputs are finite; a program needn't handle non-finite values.
Results may differ from a plain program's by a relative error of at most 0.015.
Values may be sent and summed in bfloat16 or wider, within the bound.
No kernel may reach another device: no remote copies, remote signals or barrier semaphores. Data moves between devices by JAX's collectives and lax.ppermute only.
A program may use at most 64 MiB of HBM per device.

v0:
```python
import math
import jax
import jax.numpy as jnp
from jax import lax
from jax.sharding import PartitionSpec as P

HEAD_DIM = 64
ADAPTER_RANK = 16
PAGE = 128


def request_slots(request_page_count, page_slot_table):
    slot_total = page_slot_table.shape[0]
    page_ends = jnp.cumsum(request_page_count)
    logical = jnp.arange(slot_total, dtype=jnp.int32)
    request_of = jnp.sum((logical[:, None] >= page_ends[None, :]).astype(jnp.int32), axis=1)
    matched = (page_slot_table[:, None] == logical[None, :]).astype(jnp.int32)
    return jnp.sum(matched * request_of[:, None], axis=0)


def layer_norm(values, gain_row, bias_row):
    average = jnp.mean(values, axis=-1, keepdims=True)
    centered = values - average
    variance = jnp.mean(centered * centered, axis=-1, keepdims=True)
    return centered * lax.rsqrt(variance + 1e-05) * gain_row + bias_row


def local(
    tokens,
    query_key_value_weight,
    adapter_down_weight,
    adapter_up_weight,
    attention_out_weight,
    first_norm_gain,
    first_norm_bias,
    first_feed_weight,
    first_feed_bias,
    second_feed_weight,
    second_feed_bias,
    second_norm_gain,
    second_norm_bias,
    following_qkv_weight,
    following_bias,
    request_page_count,
    page_slot_table,
    request_adapter,
):
    tok_rows = tokens.shape[0]
    mp_count = lax.axis_size("mp")
    dp_index = lax.axis_index("dp")
    mp_index = lax.axis_index("mp")
    kept_values = adapter_down_weight.shape[1] // ADAPTER_RANK
    adapter_count = kept_values * mp_count
    request_count = request_page_count.shape[0]
    slot_req = request_slots(request_page_count, page_slot_table)
    all_req = jnp.repeat(slot_req, PAGE, total_repeat_length=slot_req.shape[0] * PAGE)
    own_req = lax.dynamic_slice_in_dim(all_req, dp_index * tok_rows, tok_rows, 0)
    req_match = (own_req[:, None] == jnp.arange(request_count, dtype=jnp.int32)[None, :]).astype(
        jnp.int32
    )
    tok_adapter = jnp.sum(req_match * request_adapter[None, :], axis=1)
    grid_positions = jnp.dot(
        tokens,
        lax.all_gather(adapter_down_weight, "mp", axis=1, tiled=True),
        preferred_element_type=jnp.float32,
    )
    chosen = (tok_adapter[:, None] == jnp.arange(adapter_count, dtype=jnp.int32)[None, :]).astype(
        jnp.float32
    )
    low_rank = jnp.sum(
        grid_positions.reshape(tok_rows, adapter_count, ADAPTER_RANK) * chosen[:, :, None], axis=1
    )
    low_rank = low_rank.astype(jnp.bfloat16)
    upward_columns = lax.all_to_all(
        adapter_up_weight, "mp", split_axis=1, concat_axis=0, tiled=True
    )
    one_hot = tok_adapter[:, None] == jnp.arange(adapter_count, dtype=jnp.int32)[None, :]
    widened_rows = jnp.where(
        one_hot[:, :, None], low_rank[:, None, :], jnp.zeros((), jnp.bfloat16)
    ).reshape(tok_rows, adapter_count * ADAPTER_RANK)
    projected_rows = (
        jnp.dot(tokens, query_key_value_weight, preferred_element_type=jnp.float32)
        + jnp.dot(widened_rows, upward_columns, preferred_element_type=jnp.float32)
    ).astype(jnp.bfloat16)
    heads_dev = projected_rows.shape[1] // (3 * HEAD_DIM)
    per_head = projected_rows.reshape(tok_rows, heads_dev, 3, HEAD_DIM)
    queries = per_head[:, :, 0]
    key_value = per_head[:, :, 1:].reshape(tok_rows, heads_dev * 2 * HEAD_DIM)
    score_scale = HEAD_DIM ** (-0.5)

    def absorb_block(carry, portion, offset):
        running_max, denominator, numerator = carry
        length = portion.shape[0]
        split_rows = portion.reshape(length, heads_dev, 2, HEAD_DIM)
        key_block = split_rows[:, :, 0]
        value_block = split_rows[:, :, 1]
        key_req = lax.dynamic_slice_in_dim(all_req, offset, length, 0)
        allowed = (own_req[:, None] == key_req[None, :])[None]
        scores = (
            jnp.einsum("qhe,khe->hqk", queries, key_block, preferred_element_type=jnp.float32)
            * score_scale
        )
        block_max = jnp.max(jnp.where(allowed, scores, jnp.float32(-1e30)), axis=2)
        fresh_max = jnp.maximum(running_max, block_max)
        weights = jnp.where(allowed, jnp.exp(scores - fresh_max[:, :, None]), jnp.float32(0.0))
        shrink = jnp.exp(running_max - fresh_max)
        denominator = denominator * shrink + jnp.sum(weights, axis=2)
        numerator = numerator * shrink[:, :, None] + jnp.einsum(
            "hqk,khe->hqe",
            weights.astype(jnp.bfloat16),
            value_block,
            preferred_element_type=jnp.float32,
        )
        return (fresh_max, denominator, numerator)

    start_carry = (
        jnp.full((heads_dev, tok_rows), -1e30, jnp.float32),
        jnp.zeros((heads_dev, tok_rows), jnp.float32),
        jnp.zeros((heads_dev, tok_rows, HEAD_DIM), jnp.float32),
    )
    portion = lax.all_gather(key_value, "dp", axis=0, tiled=True)
    length = portion.shape[0]
    block_rows = math.gcd(length, 1024)

    def visit(block_index, inner):
        sub_rows = lax.dynamic_slice_in_dim(portion, block_index * block_rows, block_rows, 0)
        return absorb_block(inner, sub_rows, block_index * block_rows)

    final_max, denominator, numerator = lax.fori_loop(0, length // block_rows, visit, start_carry)
    context = (
        jnp.transpose(numerator / denominator[:, :, None], (1, 0, 2))
        .reshape(tok_rows, heads_dev * HEAD_DIM)
        .astype(jnp.bfloat16)
    )
    share_rows = tok_rows // mp_count
    row_base = mp_index * share_rows
    mixed = lax.psum(
        jnp.dot(context, attention_out_weight, preferred_element_type=jnp.float32).astype(
            jnp.bfloat16
        ),
        "mp",
    ).astype(jnp.float32)
    normed = layer_norm(
        tokens.astype(jnp.float32) + mixed, first_norm_gain, first_norm_bias
    ).astype(jnp.bfloat16)
    hidden = jax.nn.gelu(
        jnp.dot(normed, first_feed_weight, preferred_element_type=jnp.float32) + first_feed_bias,
        approximate=False,
    ).astype(jnp.bfloat16)
    feed = lax.psum(
        jnp.dot(hidden, second_feed_weight, preferred_element_type=jnp.float32).astype(
            jnp.bfloat16
        ),
        "mp",
    ).astype(jnp.float32)
    layer_full = layer_norm(
        normed.astype(jnp.float32) + feed + second_feed_bias, second_norm_gain, second_norm_bias
    ).astype(jnp.bfloat16)
    next_proj = (
        jnp.dot(layer_full, following_qkv_weight, preferred_element_type=jnp.float32)
        + following_bias
    ).astype(jnp.bfloat16)
    layer_rows = lax.dynamic_slice_in_dim(layer_full, row_base, share_rows, 0)
    return (layer_rows, next_proj)


def solution(mesh):
    placed = (
        P("dp", None),
        P(None, "mp"),
        P(None, "mp"),
        P("mp", None),
        P("mp", None),
        P(),
        P(),
        P(None, "mp"),
        P("mp"),
        P("mp", None),
        P(),
        P(),
        P(),
        P(None, "mp"),
        P("mp"),
        P(),
        P(),
        P(),
    )
    return jax.shard_map(
        local,
        mesh=mesh,
        in_specs=placed,
        out_specs=(P(("dp", "mp"), None), P("dp", "mp")),
        check_vma=False,
    )
```

profile of v0, /device:TPU:0, one launch (start us, length us, event | category | flops | bytes accessed | tf_op | source)
XLA Modules:
  0.0 462.3 jit_solution(4038813248734956425)
XLA Ops:
  10.2 6.3 %all-to-all-start = ((bf16[128,4,768]{0,2,1:T(8,128)(2,1)}), bf16[128,4,768]{0,2,1:T(8,128)(2,1)S(1)}, u32[]{:S(2)}, u32[]{:S(2)}) async-start(bf16[128,4,768]{0,2,1:T(8,128)(2,1)} %bitcast.154), calls=%async_computation | async-start | bytes 1572864 | tf_op jit(solution)/shard_map/all_to_all | solution.py:74
  19.6 4.5 compare_select_fusion.1
  24.1 5.8 %compare_reduce_fusion.56 = (pred[8192]{0:T(1024)(128)(4,1)S(1)}, pred[8192]{0:T(1024)(128)(4,1)S(1)}, pred[8192]{0:T(1024)(128)(4,1)S(1)}, pred[8192]{0:T(1024)...) fusion(s32[8192,1]{0,1:T(1,128)S(1)} %get-tuple-element.259), kind=kLoop, calls=%fused_computation.118 | loop fusion | flops 466944 | bytes 499712 | tf_op jit(solution)/shard_map/jit(_take)/gather | solution.py:56
  31.4 36.0 %select_select_fusion = s32[8192]{0:T(1024)S(1)} fusion(pred[8192]{0:T(1024)(128)(4,1)S(1)} %get-tuple-element.239, pred[8192]{0:T(1024)(128)(4,1)S(1)} %get-tuple-element.238, pred[8192]{0:T(1024)(128)(4,1)S(1)} %get-tuple-element.237, pred[8192]{0:T(1024)(128)(4,1)S(1)} %get-tuple-element.236, pred[8192]{0:T(1024)(128)(4,1)S(1)} %get-tuple-element.235, ...), kind=kLoop, calls=%fused_computation.126 | loop fusion | flops 540672 | bytes 532708 | tf_op jit(solution)/shard_map/jit(_take)/select_n | solution.py:56
  67.5 5.6 %fusion.72 = f32[1024,768]{0,1:T(8,128)} fusion(bf16[1024,1024]{1,0:T(8,128)(2,1)} %param.22, bf16[1024,768]{1,0:T(8,128)(2,1)} %param.23), kind=kOutput, calls=%fused_computation.176 | convolution fusion | flops 1610612736 | bytes 6815744 | tf_op jit(solution)/shard_map/dot_general | solution.py:82
  84.7 54.1 %all-gather.5.cloned.1.call-done = bf16[8192,512]{0,1:T(8,128)(2,1)} async-done(((bf16[1024,512]{0,1:T(8,128)(2,1)}), bf16[8192,512]{0,1:T(8,128)(2,1)}) %all-gather.5.cloned.1.call-update) | async-done | bytes 8388624 | tf_op jit(solution)/shard_map/all_gather | solution.py:121
  138.8 109.0 %while.19 = (s32[]{:T(128)}, f32[4,1024]{1,0:T(4,128)S(1)}, f32[4,1024]{1,0:T(4,128)S(1)}, f32[4,1024,64]{1,2,0:T(8,128)S(1)}, s32[1024]{0:T(1024)S(1)}, /*index...) while((s32[]{:T(128)}, f32[4,1024]{1,0:T(4,128)S(1)}, ...), condition=%wide.region_8.9_spmd.clone, body=%wide.region_5.8_spmd.clone.sunk | while | flops 1121734656 | bytes 60571836 | solution.py:129
  140.8 4.1 fusion.96
  148.5 3.8 fusion.99
  154.4 4.1 fusion.96
  162.2 3.8 fusion.99
  168.0 4.1 fusion.96
  181.6 4.1 fusion.96
  189.4 3.8 fusion.99
  195.3 4.1 fusion.96
  208.9 4.1 fusion.96
  216.7 3.8 fusion.99
  222.5 4.1 fusion.96
  230.3 3.8 fusion.99
  236.1 4.1 fusion.96
  243.9 3.8 fusion.99
  251.1 86.6 %all-reduce.3.cloned.1.call-done = bf16[1024,1024]{1,0:T(8,128)(2,1)} async-done(((bf16[1024,1024]{1,0:T(8,128)(2,1)}), bf16[1024,1024]{1,0:T(8,128)(2,1)}) %all-reduce.3.cloned.1.call-update) | async-done | bytes 2097168 | tf_op jit(solution)/shard_map/psum | solution.py:137
  344.5 15.8 %fusion.32 = bf16[1024,1024]{1,0:T(8,128)(2,1)} fusion(bf16[1024,1024]{1,0:T(8,128)(2,1)S(1)} %copy-done, f32[1024]{0:T(1024)S(1)} %copy-done.15, bf16[1024,1024]{1,0:T(8,128)(2,1)} %add_convert_fusion.1, bf16[1024,1024]{1,0:T(8,128)(2,1)} %param.29), kind=kOutput, calls=%fused_computation.56 | convolution fusion | flops 4365221888 | bytes 8392704 | tf_op jit(solution)/shard_map/dot_general | solution.py:151
  360.3 85.6 %all-reduce.5.cloned.1.call-done = bf16[1024,1024]{1,0:T(8,128)(2,1)} async-done(((bf16[1024,1024]{1,0:T(8,128)(2,1)}), bf16[1024,1024]{1,0:T(8,128)(2,1)}) %all-reduce.5.cloned.1.call-update) | async-done | bytes 2097168 | tf_op jit(solution)/shard_map/psum | solution.py:150
  (139 shorter events, 92.0 us)
Async XLA Ops:
  7.2 337.3 %copy-start = (bf16[1024,1024]{1,0:T(8,128)(2,1)S(1)}, bf16[1024,1024]{1,0:T(8,128)(2,1)}, u32[]{:S(2)}) copy-start(bf16[1024,1024]{1,0:T(8,128)(2,1)} %param.31) | copy-start | bytes 6291460
  7.2 60.2 %copy-start.13 = (s32[4]{0:T(128)S(1)}, s32[4]{0:T(128)}, u32[]{:S(2)}) copy-start(s32[4]{0:T(128)} %param.39) | copy-start | bytes 52
  7.2 68.2 %all-gather.3.cloned.1.call-start = ((), (), s32[]{:S(2)}) async-start(), calls=%async_computation.1 | async-start | bytes 1310720 | tf_op jit(solution)/shard_map/all_gather | solution.py:64
  10.2 62.9 %all-to-all-start = ((bf16[128,4,768]{0,2,1:T(8,128)(2,1)}), bf16[128,4,768]{0,2,1:T(8,128)(2,1)S(1)}, u32[]{:S(2)}, u32[]{:S(2)}) async-start(bf16[128,4,768]{0,2,1:T(8,128)(2,1)} %bitcast.154), calls=%async_computation | async-start | bytes 1572864 | tf_op jit(solution)/shard_map/all_to_all | solution.py:74
  16.5 122.3 %all-gather.5.cloned.1.call-start = ((), (), s32[]{:S(2)}) async-start(), calls=%async_computation.2 | async-start | bytes 9437184 | tf_op jit(solution)/shard_map/all_gather | solution.py:121
  73.1 0.9 copy-start.7
  75.4 3.8 copy-start.6
  80.3 1.1 copy-start.5
  82.8 254.9 %all-reduce.3.cloned.1.call-start = ((), (), s32[]{:S(2)}) async-start(), calls=%async_computation.3 | async-start | bytes 4194304 | tf_op jit(solution)/shard_map/psum | solution.py:137
  251.0 91.1 %copy-start.9 = (f32[1024]{0:T(1024)S(1)}, f32[1024]{0:T(1024)}, u32[]{:S(2)}) copy-start(f32[1024]{0:T(1024)} %param.28) | copy-start | bytes 12292
  251.0 91.1 %copy-start.10 = (f32[1024]{0:T(1024)S(1)}, f32[1024]{0:T(1024)}, u32[]{:S(2)}) copy-start(f32[1024]{0:T(1024)} %param.27) | copy-start | bytes 12292
  251.0 194.9 %all-reduce.5.cloned.1.call-start = ((), (), s32[]{:S(2)}) async-start(), calls=%async_computation.4 | async-start | bytes 4194304 | tf_op jit(solution)/shard_map/psum | solution.py:150
  337.6 3.0 copy-start.2
  337.6 3.5 copy-start.3
  342.0 2.4 copy-start.15
  344.5 101.4 %copy-start.8 = (f32[1024]{0:T(1024)S(1)}, f32[1024]{0:T(1024)}, u32[]{:S(2)}) copy-start(f32[1024]{0:T(1024)} %param.32) | copy-start | bytes 12292
  360.3 90.2 %copy-start.11 = (f32[1024]{0:T(1024)S(1)}, f32[1024]{0:T(1024)}, u32[]{:S(2)}) copy-start(f32[1024]{0:T(1024)} %param.34) | copy-start | bytes 12292
  360.3 90.2 %copy-start.12 = (f32[1024]{0:T(1024)S(1)}, f32[1024]{0:T(1024)}, u32[]{:S(2)}) copy-start(f32[1024]{0:T(1024)} %param.33) | copy-start | bytes 12292
  445.9 3.1 copy-start.1
  445.9 3.5 copy-start.4
  450.4 2.4 copy-start.14
  450.4 2.4 copy-start.16
Sparse Core Ops, SparseCore 0:
  9.6 44.6 all-gather.2
  82.9 55.8 all-gather.4
  251.1 86.4 all-reduce.2
  360.4 85.4 all-reduce.4
where the time goes:
time: 464 us; the launch traced here: 462 us
  waiting for transfers between devices  227 us (49%)
  other arithmetic  95.4 us (21%)
  matrix products  94.8 us (20%)
  local copies, waits for them, and re-layouts  24 us (5%)
  between operations  14.1 us (3%)
  starting transfers between devices  6.44 us (1%)
    psum x1, waiting for transfers between devices, local(): lax.psum(jnp.dot(context, attention_out_weight, preferred_element_type=jn...  86.6 us
    psum x1, waiting for transfers between devices, local(): lax.psum(jnp.dot(hidden, second_feed_weight, preferred_element_type=jnp.f...  85.6 us
    all_gather x1, waiting for transfers between devices, local(): portion = lax.all_gather(key_value, 'dp', axis=0, tiled=True)  54.1 us
    select_n x1, other arithmetic, local(): jnp.repeat(slot_req, PAGE, total_repeat_length=slot_req.shape[0] * PAGE)  36 us
    dot_general x8, matrix products, absorb_block(): jnp.einsum('qhe,khe->hqk', queries, key_block, preferred_element_type=jnp...  32.6 us
    dot_general x8, matrix products, absorb_block(): jnp.einsum('hqk,khe->hqe', weights.astype(jnp.bfloat16), value_block, pre...  30.5 us
    reduce_sum x8, other arithmetic, absorb_block(): denominator = denominator * shrink + jnp.sum(weights, axis=2)  29.3 us
    dot_general x1, matrix products, local(): jnp.dot(hidden, second_feed_weight, preferred_element_type=jnp.float32)  15.8 us
  transfers between devices with their start and end apart: 5, of which 3 were waited for; matrix products, arithmetic and copies ran while one was open for 13% of the time, Pallas kernels for 0%

commit v1 on v0

--- a/solution.py
+++ b/solution.py
@@ -134,11 +134,14 @@
     )
     share_rows = tok_rows // mp_count
     row_base = mp_index * share_rows
-    mixed = lax.psum(
-        jnp.dot(context, attention_out_weight, preferred_element_type=jnp.float32).astype(
-            jnp.bfloat16
+    mixed = jnp.sum(
+        lax.all_gather(
+            jnp.dot(context, attention_out_weight, preferred_element_type=jnp.float32).astype(
+                jnp.bfloat16
+            ),
+            "mp",
         ),
-        "mp",
+        axis=0,
     ).astype(jnp.float32)
     normed = layer_norm(
         tokens.astype(jnp.float32) + mixed, first_norm_gain, first_norm_bias

time: 464 us -> 553 us (1.19); the launches traced: 462 us -> 543 us
  waiting for transfers between devices: 227 us -> 289 us
  local copies, waits for them, and re-layouts: 24 us -> 34.2 us
  other arithmetic: 95.4 us -> 103 us
    all_gather x0 -> x1, waiting for transfers between devices: none -> 150 us  [local(): lax.all_gather(jnp.dot(context, attention_out_weight, preferred_element_t...]
    psum x1 -> x0, waiting for transfers between devices: 86.6 us -> none  [local(): lax.psum(jnp.dot(context, attention_out_weight, preferred_element_type=jn...]
    slice x1, local copies, waits for them, and re-layouts: 1.31 us -> 11.5 us  [local(): key_value = per_head[:, :, 1:].reshape(tok_rows, heads_dev * 2 * HEAD_DIM)]
    reduce_sum x0 -> x1, other arithmetic: none -> 7.52 us  [local(): jnp.sum(lax.all_gather(jnp.dot(context, attention_out_weight, preferred_e...]
  transfers between devices with their start and end apart: 5 -> 5, of which waited for: 3 -> 3; matrix products, arithmetic and copies ran while one was open for 13% -> 11% of each run, Pallas kernels for 0% -> 0%
where the time goes in v1:
time: 553 us; the launch traced here: 543 us
  waiting for transfers between devices  289 us (52%)
  other arithmetic  103 us (19%)
  matrix products  94.9 us (17%)
  local copies, waits for them, and re-layouts  34.2 us (6%)
  between operations  14.4 us (3%)
  starting transfers between devices  6.44 us (1%)
    all_gather x1, waiting for transfers between devices, local(): lax.all_gather(jnp.dot(context, attention_out_weight, preferred_element_t...  150 us
    psum x1, waiting for transfers between devices, local(): lax.psum(jnp.dot(hidden, second_feed_weight, preferred_element_type=jnp.f...  84.9 us
    all_gather x1, waiting for transfers between devices, local(): portion = lax.all_gather(key_value, 'dp', axis=0, tiled=True)  54.1 us
    select_n x1, other arithmetic, local(): jnp.repeat(slot_req, PAGE, total_repeat_length=slot_req.shape[0] * PAGE)  36 us
    dot_general x8, matrix products, absorb_block(): jnp.einsum('qhe,khe->hqk', queries, key_block, preferred_element_type=jnp...  32.6 us
    dot_general x8, matrix products, absorb_block(): jnp.einsum('hqk,khe->hqe', weights.astype(jnp.bfloat16), value_block, pre...  30.5 us
    reduce_sum x8, other arithmetic, absorb_block(): denominator = denominator * shrink + jnp.sum(weights, axis=2)  29.3 us
    dot_general x1, matrix products, local(): jnp.dot(hidden, second_feed_weight, preferred_element_type=jnp.float32)  15.8 us
  transfers between devices with their start and end apart: 5, of which 3 were waited for; matrix products, arithmetic and copies ran while one was open for 11% of the time, Pallas kernels for 0%

profile of v1, /device:TPU:0, one launch (start us, length us, event | category | flops | bytes accessed | tf_op | source)
XLA Modules:
  0.0 542.9 jit_solution(2007371296714224089)
XLA Ops:
  10.2 6.3 %all-to-all-start = ((bf16[128,4,768]{0,2,1:T(8,128)(2,1)}), bf16[128,4,768]{0,2,1:T(8,128)(2,1)S(1)}, u32[]{:S(2)}, u32[]{:S(2)}) async-start(bf16[128,4,768]{0,2,1:T(8,128)(2,1)} %bitcast.156), calls=%async_computation | async-start | bytes 1572864 | tf_op jit(solution)/shard_map/all_to_all | solution.py:74
  19.6 4.5 compare_select_fusion.1
  24.1 5.8 %compare_reduce_fusion.56 = (pred[8192]{0:T(1024)(128)(4,1)S(1)}, pred[8192]{0:T(1024)(128)(4,1)S(1)}, pred[8192]{0:T(1024)(128)(4,1)S(1)}, pred[8192]{0:T(1024)...) fusion(s32[8192,1]{0,1:T(1,128)S(1)} %get-tuple-element.259), kind=kLoop, calls=%fused_computation.118 | loop fusion | flops 466944 | bytes 499712 | tf_op jit(solution)/shard_map/jit(_take)/gather | solution.py:56
  31.4 36.0 %select_select_fusion = s32[8192]{0:T(1024)S(1)} fusion(pred[8192]{0:T(1024)(128)(4,1)S(1)} %get-tuple-element.239, pred[8192]{0:T(1024)(128)(4,1)S(1)} %get-tuple-element.238, pred[8192]{0:T(1024)(128)(4,1)S(1)} %get-tuple-element.237, pred[8192]{0:T(1024)(128)(4,1)S(1)} %get-tuple-element.236, pred[8192]{0:T(1024)(128)(4,1)S(1)} %get-tuple-element.235, ...), kind=kLoop, calls=%fused_computation.126 | loop fusion | flops 540672 | bytes 532708 | tf_op jit(solution)/shard_map/jit(_take)/select_n | solution.py:56
  67.5 5.5 %fusion.72 = f32[1024,768]{0,1:T(8,128)} fusion(bf16[1024,1024]{1,0:T(8,128)(2,1)} %param.22, bf16[1024,768]{1,0:T(8,128)(2,1)} %param.23), kind=kOutput, calls=%fused_computation.176 | convolution fusion | flops 1610612736 | bytes 6815744 | tf_op jit(solution)/shard_map/dot_general | solution.py:82
  81.4 11.5 %slice.107 = bf16[1024,4,2,64]{0,3,2,1:T(8,128)(2,1)} slice(bf16[1024,4,3,64]{0,3,2,1:T(8,128)(2,1)S(1)} %bitcast.150), slice={[0:1024], [0:4], [1:3], [0:64]} | slice | bytes 2097152 | tf_op jit(solution)/shard_map/slice | solution.py:88
  94.9 54.1 %all-gather.7.cloned.1.call-done = bf16[8192,512]{0,1:T(8,128)(2,1)} async-done(((bf16[1024,512]{0,1:T(8,128)(2,1)}), bf16[8192,512]{0,1:T(8,128)(2,1)}) %all-gather.7.cloned.1.call-update) | async-done | bytes 8388624 | tf_op jit(solution)/shard_map/all_gather | solution.py:121
  149.0 109.0 %while.19 = (s32[]{:T(128)}, f32[4,1024]{1,0:T(4,128)S(1)}, f32[4,1024]{1,0:T(4,128)S(1)}, f32[4,1024,64]{1,2,0:T(8,128)S(1)}, s32[1024]{0:T(1024)S(1)}, /*index...) while((s32[]{:T(128)}, f32[4,1024]{1,0:T(4,128)S(1)}, ...), condition=%wide.region_8.9_spmd.clone, body=%wide.region_5.8_spmd.clone.sunk | while | flops 1121734656 | bytes 60571836 | solution.py:129
  151.0 4.1 fusion.96
  164.6 4.1 fusion.96
  178.2 4.1 fusion.96
  186.0 3.8 fusion.99
  191.9 4.1 fusion.96
  205.5 4.1 fusion.96
  219.1 4.1 fusion.96
  226.9 3.8 fusion.99
  232.7 4.1 fusion.96
  240.5 3.8 fusion.99
  246.4 4.1 fusion.96
  254.1 3.8 fusion.99
  261.4 149.7 %all-gather.9.cloned.1.call-done = bf16[4096,1024]{1,0:T(8,128)(2,1)} async-done(((bf16[1024,1024]{1,0:T(8,128)(2,1)}), bf16[4096,1024]{1,0:T(8,128)(2,1)}) %all-gather.9.cloned.1.call-update) | async-done | bytes 8388624 | tf_op jit(solution)/shard_map/all_gather | solution.py:138
  411.1 7.5 %reduce_sum.101 = bf16[1024,1024]{1,0:T(8,128)(2,1)} reduce(bf16[4,1024,1024]{2,1,0:T(8,128)(2,1)} %bitcast.149, bf16[]{:T(256)} %constant.193.clone.1), dimensions={0}, to_apply=%region_9.10 | reduce | flops 3145728 | bytes 10485762 | tf_op jit(solution)/shard_map/reduce_sum | solution.py:137
  425.5 15.8 %fusion.32 = bf16[1024,1024]{1,0:T(8,128)(2,1)} fusion(bf16[1024,1024]{1,0:T(8,128)(2,1)S(1)} %copy-done, f32[1024]{0:T(1024)S(1)} %copy-done.15, bf16[1024,1024]{1,0:T(8,128)(2,1)} %add_convert_fusion.1, bf16[1024,1024]{1,0:T(8,128)(2,1)} %param.29), kind=kOutput, calls=%fused_computation.56 | convolution fusion | flops 4365221888 | bytes 8392704 | tf_op jit(solution)/shard_map/dot_general | solution.py:154
  441.3 84.9 %all-reduce.2.cloned.1.call-done = bf16[1024,1024]{1,0:T(8,128)(2,1)} async-done(((bf16[1024,1024]{1,0:T(8,128)(2,1)}), bf16[1024,1024]{1,0:T(8,128)(2,1)}) %all-reduce.2.cloned.1.call-update) | async-done | bytes 2097168 | tf_op jit(solution)/shard_map/psum | solution.py:153
  (140 shorter events, 98.4 us)
Async XLA Ops:
  7.2 418.3 %copy-start = (bf16[1024,1024]{1,0:T(8,128)(2,1)S(1)}, bf16[1024,1024]{1,0:T(8,128)(2,1)}, u32[]{:S(2)}) copy-start(bf16[1024,1024]{1,0:T(8,128)(2,1)} %param.31) | copy-start | bytes 6291460
  7.2 60.2 %copy-start.13 = (s32[4]{0:T(128)S(1)}, s32[4]{0:T(128)}, u32[]{:S(2)}) copy-start(s32[4]{0:T(128)} %param.39) | copy-start | bytes 52
  7.2 68.2 %all-gather.5.cloned.1.call-start = ((), (), s32[]{:S(2)}) async-start(), calls=%async_computation.1 | async-start | bytes 1310720 | tf_op jit(solution)/shard_map/all_gather | solution.py:64
  10.2 62.9 %all-to-all-start = ((bf16[128,4,768]{0,2,1:T(8,128)(2,1)}), bf16[128,4,768]{0,2,1:T(8,128)(2,1)S(1)}, u32[]{:S(2)}, u32[]{:S(2)}) async-start(bf16[128,4,768]{0,2,1:T(8,128)(2,1)} %bitcast.156), calls=%async_computation | async-start | bytes 1572864 | tf_op jit(solution)/shard_map/all_to_all | solution.py:74
  16.5 132.5 %all-gather.7.cloned.1.call-start = ((), (), s32[]{:S(2)}) async-start(), calls=%async_computation.2 | async-start | bytes 9437184 | tf_op jit(solution)/shard_map/all_gather | solution.py:121
  73.1 0.9 copy-start.7
  75.4 3.8 copy-start.6
  80.3 1.1 copy-start.5
  93.0 318.1 %all-gather.9.cloned.1.call-start = ((), (), s32[]{:S(2)}) async-start(), calls=%async_computation.4 | async-start | bytes 10485760 | tf_op jit(solution)/shard_map/all_gather | solution.py:138
  261.3 264.8 %all-reduce.2.cloned.1.call-start = ((), (), s32[]{:S(2)}) async-start(), calls=%async_computation.3 | async-start | bytes 4194304 | tf_op jit(solution)/shard_map/psum | solution.py:153
  418.6 3.0 copy-start.2
  418.6 3.5 copy-start.3
  418.6 4.4 copy-start.9
  418.6 4.4 copy-start.10
  423.0 2.4 copy-start.15
  425.5 100.7 %copy-start.8 = (f32[1024]{0:T(1024)S(1)}, f32[1024]{0:T(1024)}, u32[]{:S(2)}) copy-start(f32[1024]{0:T(1024)} %param.32) | copy-start | bytes 12292
  441.2 89.5 %copy-start.11 = (f32[1024]{0:T(1024)S(1)}, f32[1024]{0:T(1024)}, u32[]{:S(2)}) copy-start(f32[1024]{0:T(1024)} %param.34) | copy-start | bytes 12292
  441.3 89.4 %copy-start.12 = (f32[1024]{0:T(1024)S(1)}, f32[1024]{0:T(1024)}, u32[]{:S(2)}) copy-start(f32[1024]{0:T(1024)} %param.33) | copy-start | bytes 12292
  526.1 3.1 copy-start.1
  526.1 3.5 copy-start.4
  530.7 2.4 copy-start.14
  530.7 2.4 copy-start.16
Sparse Core Ops, SparseCore 0:
  9.6 44.6 all-gather.4
  93.1 55.8 all-gather.6
  261.4 149.6 all-gather.8
  441.4 84.7 all-reduce.1
